TPU v7x, 512 devices: a whole 4x8x8 slice. The times are simulated.
512 devices in a mesh: seq: 64 (over z, y), req: 8 (over x, core).
Axes of the slice: x: 4, y: 8, z: 8, core: 2. Of those that a mesh axis runs over, the one named last changes fastest.
Arguments:
- hidden_in: bfloat16 [128, 4, 2048], P('req'), may hold values from -6 to 6
- attn_gain: float32 [2048], replicated, may hold values from 0.5 to 1.5
- q_gain: float32 [256], replicated, may hold values from 0.5 to 1.5
- k_gain: float32 [256], replicated, may hold values from 0.5 to 1.5
- post_attn_gain: float32 [2048], replicated, may hold values from 0.5 to 1.5
- ffn_gain: float32 [2048], replicated, may hold values from 0.5 to 1.5
- post_ffn_gain: float32 [2048], replicated, may hold values from 0.5 to 1.5
- w_qkv: bfloat16 [2048, 3072], P('seq', 'req'), may hold values from -0.125 to 0.125
- w_out: bfloat16 [2048, 2048], P('seq', 'req'), may hold values from -0.125 to 0.125
- w_gate: bfloat16 [2048, 8192], P('req', 'seq'), may hold values from -0.125 to 0.125
- w_up: bfloat16 [2048, 8192], P('req', 'seq'), may hold values from -0.125 to 0.125
- w_down: bfloat16 [8192, 2048], P('seq', 'req'), may hold values from -0.0625 to 0.0625
- prompt_keys: bfloat16 [16, 8192, 512], P('req', 'seq')
- prompt_values: bfloat16 [16, 8192, 512], P('req', 'seq'), may hold values from -6 to 6
- tail_keys: bfloat16 [8, 16384, 512], P('req', 'seq')
- tail_values: bfloat16 [8, 16384, 512], P('req', 'seq'), may hold values from -6 to 6
- group_of: int32 [128], P('req'), may hold values from 0 to 15, as said below
- prompt_lengths: int32 [16], P('req'), may hold values from 1 to 8192
- tail_lengths: int32 [128], P('req'), may hold values from 1 to 1024
- page_table: int32 [8, 1024], P('req'), may hold values from 0 to 1023, each once within a row
Outputs:
- layer_out: bfloat16 [128, 4, 2048], P('req')
Inputs may be any that keep to these rules, and one draw needn't show every extreme that they name: `group_of`: request i belongs to one of the 2 groups i // 16 * 2 to i // 16 * 2 + 1 of its own block of requests. `page_table`: each row lists every pool page of its index of req once; entry j * 64 + p is the pool page of page p of the j-th request of that block.
All inputs are finite; a program needn't handle non-finite values.
Results may differ from a plain program's by a relative error of at most 0.012.
The roundings to bfloat16 on the way count: a program that leaves them out, or rounds other values in their place, can miss the bound.
Values may be sent and summed in bfloat16 or wider, within the bound.
A program may use at most 128 MiB of HBM per device.

v0:
```python
import jax
import jax.numpy as jnp
from jax import lax
from jax.sharding import PartitionSpec as P

D = 2048
H = 8
KV = 2
HD = 256
PAGE = 16
QKV = 3072


EPSILON = 1e-06
NEGATIVE = -1e30


def normalize(values):
    return values * lax.rsqrt(jnp.mean(values * values, axis=-1, keepdims=True) + EPSILON)


def on_device(
    hidden_in,
    attn_gain,
    q_gain,
    k_gain,
    post_attn_gain,
    ffn_gain,
    post_ffn_gain,
    w_qkv,
    w_out,
    w_gate,
    w_up,
    w_down,
    prompt_keys,
    prompt_values,
    tail_keys,
    tail_values,
    group_of,
    prompt_lengths,
    tail_lengths,
    page_table,
):
    seq_index = lax.axis_index("seq")
    rows_req = hidden_in.shape[0]
    step_count = hidden_in.shape[1]
    group_size = H // KV
    tokens = rows_req * step_count
    hidden = hidden_in.astype(jnp.float32)
    normed = (normalize(hidden) * attn_gain).astype(jnp.bfloat16)
    in_rows = w_qkv.shape[0]
    normed_cols = lax.dynamic_slice_in_dim(normed, seq_index * in_rows, in_rows, 2).reshape(
        tokens, in_rows
    )
    qkv_full, out_full, gate_full, up_full, down_full = (
        lax.all_gather(w_qkv, "req", axis=1, tiled=True),
        lax.all_gather(w_out, "req", axis=1, tiled=True),
        lax.all_gather(w_gate, "req", axis=0, tiled=True),
        lax.all_gather(w_up, "req", axis=0, tiled=True),
        lax.all_gather(w_down, "req", axis=1, tiled=True),
    )
    qkv_part = jnp.dot(normed_cols, qkv_full, preferred_element_type=jnp.float32)
    projected = lax.psum(qkv_part, "seq").reshape(rows_req, step_count, QKV)
    queries = (
        normalize(projected[..., : H * HD].reshape(rows_req, step_count, H, HD)) * q_gain
    ).astype(jnp.bfloat16)
    keys_new = (
        normalize(projected[..., H * HD : (H + KV) * HD].reshape(rows_req, step_count, KV, HD))
        * k_gain
    ).astype(jnp.bfloat16)
    values_new = normalize(
        projected[..., (H + KV) * HD :].reshape(rows_req, step_count, KV, HD)
    ).astype(jnp.bfloat16)
    query_groups = queries.reshape(rows_req, step_count, KV, group_size, HD)
    group_count = prompt_keys.shape[0]
    prompt_span = prompt_keys.shape[1]
    cache_keys = prompt_keys.reshape(group_count, prompt_span, KV, HD)
    cache_values = prompt_values.reshape(group_count, prompt_span, KV, HD)
    member = (group_of % group_count)[:, None] == jnp.arange(group_count, dtype=jnp.int32)[None, :]
    prompt_pos = seq_index * prompt_span + jnp.arange(prompt_span, dtype=jnp.int32)
    prompt_live = prompt_pos[None, :] < prompt_lengths[:, None]
    prompt_mask = (member[:, :, None] & prompt_live[None, :, :])[:, None, None, None, :, :]
    prompt_scores = jnp.einsum(
        "rskgd,cpkd->rskgcp", query_groups, cache_keys, preferred_element_type=jnp.float32
    )
    prompt_scores = jnp.where(prompt_mask, prompt_scores, NEGATIVE)
    pool_rows = tail_keys.shape[1]
    slot_count = pool_rows // PAGE
    table_row = page_table[0]
    table_len = table_row.shape[0]
    tail_pages = table_len // rows_req
    slot_ids = seq_index * slot_count + jnp.arange(slot_count, dtype=jnp.int32)
    matches = table_row[None, :] == slot_ids[:, None]
    entries = jnp.sum(
        jnp.where(matches, jnp.arange(table_len, dtype=jnp.int32)[None, :], 0), axis=1
    )
    owners = jnp.repeat(entries // tail_pages, PAGE)
    tail_pos = jnp.repeat(entries % tail_pages, PAGE) * PAGE + jnp.tile(
        jnp.arange(PAGE, dtype=jnp.int32), slot_count
    )
    tail_mask = (owners[None, :] == jnp.arange(rows_req, dtype=jnp.int32)[:, None]) & (
        tail_pos[None, :] < tail_lengths[:, None]
    )
    tail_mask = tail_mask[:, None, None, None, :]
    pool_keys = tail_keys[0].reshape(pool_rows, KV, HD)
    pool_values = tail_values[0].reshape(pool_rows, KV, HD)
    tail_scores = jnp.einsum(
        "rskgd,pkd->rskgp", query_groups, pool_keys, preferred_element_type=jnp.float32
    )
    tail_scores = jnp.where(tail_mask, tail_scores, NEGATIVE)
    block_top = jnp.maximum(jnp.max(prompt_scores, axis=(4, 5)), jnp.max(tail_scores, axis=4))
    prompt_probs = jnp.where(prompt_mask, jnp.exp(prompt_scores - block_top[..., None, None]), 0.0)
    tail_probs = jnp.where(tail_mask, jnp.exp(tail_scores - block_top[..., None]), 0.0)
    block_total = jnp.sum(prompt_probs, axis=(4, 5)) + jnp.sum(tail_probs, axis=4)
    block_accum = jnp.einsum(
        "rskgcp,cpkd->rskgd",
        prompt_probs.astype(jnp.bfloat16),
        cache_values,
        preferred_element_type=jnp.float32,
    )
    block_accum = block_accum + jnp.einsum(
        "rskgp,pkd->rskgd",
        tail_probs.astype(jnp.bfloat16),
        pool_values,
        preferred_element_type=jnp.float32,
    )
    new_scores = jnp.einsum(
        "rskgd,rukd->rskgu", query_groups, keys_new, preferred_element_type=jnp.float32
    )
    causal = (jnp.arange(step_count)[:, None] >= jnp.arange(step_count)[None, :])[
        None, :, None, None, :
    ]
    new_scores = jnp.where(causal, new_scores, NEGATIVE)
    attn_rows_dev = w_out.shape[0]
    top_max = lax.pmax(block_top, "seq")
    rescale = jnp.exp(block_top - top_max)
    total_sum, accumulated = lax.psum(
        (block_total * rescale, block_accum * rescale[..., None]), "seq"
    )
    highest = jnp.maximum(top_max, jnp.max(new_scores, axis=4))
    carried = jnp.exp(top_max - highest)
    new_probs = jnp.where(causal, jnp.exp(new_scores - highest[..., None]), 0.0)
    denominator = total_sum * carried + jnp.sum(new_probs, axis=4)
    numerator = accumulated * carried[..., None] + jnp.einsum(
        "rskgu,rukd->rskgd", new_probs, values_new.astype(jnp.float32)
    )
    attention = (
        (numerator / denominator[..., None])
        .astype(jnp.bfloat16)
        .reshape(rows_req, step_count, H * HD)
    )
    attention_cols = lax.dynamic_slice_in_dim(
        attention, seq_index * attn_rows_dev, attn_rows_dev, 2
    ).reshape(tokens, attn_rows_dev)
    out_part = jnp.dot(attention_cols, out_full, preferred_element_type=jnp.float32)
    attn_out = lax.psum(out_part, "seq")
    residual = hidden.reshape(tokens, D) + normalize(attn_out) * post_attn_gain
    ffn_in = (normalize(residual) * ffn_gain).astype(jnp.bfloat16)
    gate_out = jnp.dot(ffn_in, gate_full, preferred_element_type=jnp.float32)
    up_out = jnp.dot(ffn_in, up_full, preferred_element_type=jnp.float32)
    activated = (jax.nn.gelu(gate_out, approximate=True) * up_out).astype(jnp.bfloat16)
    down_part = jnp.dot(activated, down_full, preferred_element_type=jnp.float32)
    down_out = lax.psum(down_part, "seq")
    layer_out = residual + normalize(down_out) * post_ffn_gain
    return layer_out.astype(jnp.bfloat16).reshape(rows_req, step_count, D)


def solution(mesh):
    return jax.shard_map(
        on_device,
        mesh=mesh,
        in_specs=(
            P("req", None, None),
            P(),
            P(),
            P(),
            P(),
            P(),
            P(),
            P("seq", "req"),
            P("seq", "req"),
            P("req", "seq"),
            P("req", "seq"),
            P("seq", "req"),
            P("req", "seq", None),
            P("req", "seq", None),
            P("req", "seq", None),
            P("req", "seq", None),
            P("req"),
            P("req"),
            P("req"),
            P("req", None),
        ),
        out_specs=P("req", None, None),
        check_vma=False,
    )
```

profile of v0, /device:TPU:6, one launch (start us, length us, event | category | flops | bytes accessed | tf_op | source)
XLA Modules:
  0.0 1219.4 jit_solution(10066826392859031519)
XLA Ops:
  6.5 1.1 convert_element_type.35
  7.6 0.2 multiply_reduce_fusion.3
  7.8 0.7 copy-done.11
  8.6 15.5 %all_gather.15 = bf16[32,3072]{1,0:T(8,128)(2,1)S(1)} all-gather(bf16[32,384]{1,0:T(8,128)(2,1)S(1)} %copy-done.11), channel_id=1, replica_groups=mesh['seq'=64,'req'=8] {'req'}, dimensions={1}, use_global_device_ids=true | all-gather | bytes 221184 | tf_op jit(solution)/shard_map/all_gather | solution.py:56
  24.1 0.8 dynamic-slice
  24.8 0.1 fusion.48
  24.9 0.2 fusion.68
  25.2 0.2 reshape.248
  25.4 1.4 copy.120
  26.9 0.6 copy-done.15
  27.4 0.2 select_reduce_fusion
  27.7 13.1 %all_gather.16 = bf16[32,2048]{1,0:T(8,128)(2,1)S(1)} all-gather(bf16[32,256]{1,0:T(8,128)(2,1)S(1)} %copy-done.12), channel_id=1, replica_groups=mesh['seq'=64,'req'=8] {'req'}, dimensions={1}, use_global_device_ids=true | all-gather | bytes 147456 | tf_op jit(solution)/shard_map/all_gather | solution.py:57
  41.1 0.9 copy-done.4
  42.1 0.9 copy-done.5
  43.0 0.9 copy-done.6
  44.0 0.6 copy-done.20
  44.8 0.6 copy-done.19
  45.4 142.4 %all-reduce.5.cloned.1.call-done = f32[16,4,3072]{2,0,1:T(8,128)} async-done(((f32[16,4,3072]{2,0,1:T(8,128)}), f32[16,4,3072]{2,0,1:T(8,128)}) %all-reduce.5.cloned.1.call-update) | async-done | bytes 786448 | tf_op jit(solution)/shard_map/psum | solution.py:63
  187.8 1.1 slice_multiply_fusion
  188.9 0.2 copy.162
  189.1 0.1 reduce_sum.100
  189.3 0.4 reshape.249
  189.7 0.7 copy-done.16
  190.4 0.2 fusion.10
  190.6 0.4 fusion.65
  191.0 0.3 fusion.66
  191.4 277.1 %pmax.7 = f32[16,4,2,4]{0,3,1,2:T(4,128)S(1)} all-reduce(f32[16,4,2,4]{0,3,1,2:T(4,128)S(1)} %max.16), channel_id=1, replica_groups=mesh['seq'=64,'req'=8] {'seq'}, use_global_device_ids=true, to_apply=%region_6.7 | all-reduce | flops 512 | bytes 4096 | tf_op jit(solution)/shard_map/pmax | solution.py:135
  468.5 0.3 fusion.13
  468.8 0.3 fusion.11
  469.1 1.0 fusion.64
  470.2 0.1 multiply_reduce_fusion.5
  470.4 0.6 copy-done.17
  471.0 0.1 fusion.35
  471.2 1.3 fusion.67
  472.5 0.1 copy.131
  472.6 0.1 copy.132
  472.8 0.3 fusion.30
  473.0 0.1 copy.136
  473.2 273.9 %psum.37 = f32[16,4,2,4]{0,3,1,2:T(4,128)S(1)} all-reduce(f32[16,4,2,4]{0,3,1,2:T(4,128)S(1)} %bitcast.93), channel_id=1, replica_groups=mesh['seq'=64,'req'=8] {'seq'}, use_global_device_ids=true, to_apply=%region_13.14 | all-reduce | flops 512 | bytes 4096 | tf_op jit(solution)/shard_map/psum | solution.py:137
  747.1 0.3 convolution_bitcast_fusion
  747.4 1.1 fusion.3
  748.7 0.1 multiply_reduce_fusion.4
  748.9 0.1 fusion.36
  749.0 0.4 fusion.31
  749.4 149.1 %all-reduce.7.cloned.1.call-done = f32[16,4,2,4,256]{4,0,3,1,2:T(8,128)} async-done(((f32[16,4,2,4,256]{4,0,3,1,2:T(8,128)}), f32[16,4,2,4,256]{4,0,3,1,2:T(8,128)}) %all-reduce.7.cloned.1.call-update) | async-done | bytes 524304 | tf_op jit(solution)/shard_map/psum | solution.py:137
  898.5 1.4 fusion.8
  899.9 0.1 copy.137
  900.1 0.2 reshape.254
  900.3 1.0 fusion.69
  901.4 0.8 copy-done.7
  902.2 13.1 %all_gather.17 = bf16[2048,128]{1,0:T(8,128)(2,1)S(1)} all-gather(bf16[256,128]{1,0:T(8,128)(2,1)S(1)} %copy-done.7), channel_id=1, replica_groups=mesh['seq'=64,'req'=8] {'req'}, dimensions={0}, use_global_device_ids=true | all-gather | bytes 589824 | tf_op jit(solution)/shard_map/all_gather | solution.py:58
  915.3 0.8 copy-done.8
  916.1 13.2 %all_gather.18 = bf16[2048,128]{1,0:T(8,128)(2,1)S(1)} all-gather(bf16[256,128]{1,0:T(8,128)(2,1)S(1)} %copy-done.8), channel_id=1, replica_groups=mesh['seq'=64,'req'=8] {'req'}, dimensions={0}, use_global_device_ids=true | all-gather | bytes 589824 | tf_op jit(solution)/shard_map/all_gather | solution.py:59
  929.4 13.2 %all_gather.19 = bf16[128,2048]{1,0:T(8,128)(2,1)S(1)} all-gather(bf16[128,256]{1,0:T(8,128)(2,1)S(1)} %copy-done.9), channel_id=1, replica_groups=mesh['seq'=64,'req'=8] {'req'}, dimensions={1}, use_global_device_ids=true | all-gather | bytes 589824 | tf_op jit(solution)/shard_map/all_gather | solution.py:60
  942.6 111.9 %all-reduce.9.cloned.1.call-done = f32[64,2048]{1,0:T(8,128)} async-done(((f32[64,2048]{1,0:T(8,128)}), f32[64,2048]{1,0:T(8,128)}) %all-reduce.9.cloned.1.call-update) | async-done | bytes 524304 | tf_op jit(solution)/shard_map/psum | solution.py:156
  1054.5 1.2 multiply_reduce_fusion.2
  1055.8 0.3 multiply_reduce_fusion.1
  1056.1 0.4 copy-done.10
  1056.5 0.3 fusion.63
  1056.8 1.3 fusion.6
  1058.1 152.6 %all-reduce.11.cloned.1.call-done = f32[64,2048]{1,0:T(8,128)} async-done(((f32[64,2048]{1,0:T(8,128)}), f32[64,2048]{1,0:T(8,128)}) %all-reduce.11.cloned.1.call-update) | async-done | bytes 524304 | tf_op jit(solution)/shard_map/psum | solution.py:163
  1210.7 1.2 multiply_reduce_fusion
  1211.9 0.1 add_convert_fusion
  1212.1 0.8 reshape.256
  (70 shorter events, 1.6 us)
Async XLA Ops:
  6.5 181.3 %all-reduce.5.cloned.1.call-start = ((), (), s32[]{:S(2)}) async-start(), calls=%async_computation | async-start | bytes 1572864 | tf_op jit(solution)/shard_map/psum | solution.py:63
  6.5 1.1 copy-start
  7.8 0.7 copy-start.11
  26.8 0.7 copy-start.15
  26.8 0.9 copy-start.18
  26.8 14.3 %copy-start.3 = (bf16[1,256,512]{2,1,0:T(8,128)(2,1)S(1)}, bf16[1,256,512]{2,1,0:T(8,128)(2,1)}, u32[]{:S(2)}) copy-start(bf16[1,256,512]{2,1,0:T(8,128)(2,1)} %param.34) | copy-start | bytes 786436
  26.8 0.9 copy-start.12
  26.8 871.7 %all-reduce.7.cloned.1.call-start = ((), (), s32[]{:S(2)}) async-start(), calls=%async_computation.1 | async-start | bytes 1048576 | tf_op jit(solution)/shard_map/psum | solution.py:137
  41.0 1.0 copy-start.4
  42.0 1.0 copy-start.5
  43.0 0.9 copy-start.6
  44.0 0.7 copy-start.20
  44.7 0.7 copy-start.19
  189.7 0.7 copy-start.16
  470.3 0.7 copy-start.17
  748.5 306.0 %all-reduce.9.cloned.1.call-start = ((), (), s32[]{:S(2)}) async-start(), calls=%async_computation.2 | async-start | bytes 1048576 | tf_op jit(solution)/shard_map/psum | solution.py:156
  901.4 0.8 copy-start.7
  901.4 309.3 %all-reduce.11.cloned.1.call-start = ((), (), s32[]{:S(2)}) async-start(), calls=%async_computation.3 | async-start | bytes 1048576 | tf_op jit(solution)/shard_map/psum | solution.py:163
  915.3 0.8 copy-start.8
  916.1 13.2 %copy-start.9 = (bf16[128,256]{1,0:T(8,128)(2,1)S(1)}, bf16[128,256]{1,0:T(8,128)(2,1)}, u32[]{:S(2)}) copy-start(bf16[128,256]{1,0:T(8,128)(2,1)} %param.31) | copy-start | bytes 196612
  929.4 126.4 %copy-start.13 = (f32[2048]{0:T(1024)S(1)}, f32[2048]{0:T(1024)}, u32[]{:S(2)}) copy-start(f32[2048]{0:T(1024)} %param.24) | copy-start | bytes 24580
  1054.5 1.3 copy-start.2
  1055.8 0.7 copy-start.10
  1058.1 153.8 %copy-start.14 = (f32[2048]{0:T(1024)S(1)}, f32[2048]{0:T(1024)}, u32[]{:S(2)}) copy-start(f32[2048]{0:T(1024)} %param.26) | copy-start | bytes 24580
  1210.7 1.3 copy-start.1
Sparse Core Ops, SparseCore 0:
  26.9 160.8 all-reduce.4
  748.6 149.8 all-reduce.6
  902.1 152.4 all-reduce.8
  1058.2 152.3 all-reduce.10
where the time goes:
time: 1220 us
  blocking collectives  619 us (51%)
  waiting for transfers between devices  556 us (46%)
  local copies, waits for them, and re-layouts  14.7 us (1%)
  between operations  13.5 us (1%)
    pmax x1, blocking collectives, on_device(): top_max = lax.pmax(block_top, 'seq')  277 us
    psum x1, blocking collectives, on_device(): lax.psum((block_total * rescale, block_accum * rescale[..., None]), 'seq')  274 us
    psum x1, waiting for transfers between devices, on_device(): down_out = lax.psum(down_part, 'seq')  153 us
    psum x1, waiting for transfers between devices, on_device(): lax.psum((block_total * rescale, block_accum * rescale[..., None]), 'seq')  149 us
    psum x1, waiting for transfers between devices, on_device(): projected = lax.psum(qkv_part, 'seq').reshape(rows_req, step_count, QKV)  142 us
    psum x1, waiting for transfers between devices, on_device(): attn_out = lax.psum(out_part, 'seq')  112 us
  transfers between devices with their start and end apart: 4, of which 4 were waited for; matrix products, arithmetic and copies ran while one was open for 0% of the time, Pallas kernels for 0%

commit v1 on v0

v1 whole, which is shorter than its diff:
```python
import jax
import jax.numpy as jnp
from jax import lax
from jax.experimental import pallas as pl
from jax.experimental.pallas import tpu as pltpu
from jax.sharding import PartitionSpec as P

MESH = pl.DeviceIdType.MESH
D = 2048
H = 8
KV = 2
HD = 256
PAGE = 16
QKV = 3072
NZ = 8
NY = 8
NS = 64
NR = 8
T = 64
STEPS = 4
REQS = 16
LANES = 128
DR = D // LANES
QR = QKV // LANES
EPSILON = 1e-06
NEGATIVE = -1e30
F32 = jnp.float32
BF16 = jnp.bfloat16
NT = (((1,), (1,)), ((), ()))


def iota(shape, dim):
    return lax.broadcasted_iota(jnp.int32, shape, dim)


def row_norm(row):
    total = jnp.sum(jnp.sum(row * row, axis=1, keepdims=True), axis=0, keepdims=True)
    return row * lax.rsqrt(total / D + EPSILON)


def kernel(
    hid_hbm, again_hbm, qgain_hbm, kgain_hbm, pagain_hbm, fgain_hbm, pfgain_hbm,
    wqkv_ref, wout_ref, wgate_ref, wup_ref, wdown_ref,
    pk_ref, pv_ref, tk_ref, tv_ref,
    grp_hbm, plen_hbm, tlen_hbm, table_hbm,
    out_ref,
    hid_ref, again_ref, qgain_ref, kgain_ref, pagain_ref, fgain_ref, pfgain_ref,
    grp_ref, plen_ref, tlen_ref, table_ref,
    hf, hid3, nb, kbuf, vbuf, maskf,
    wown, wq, wo, wg, wu, wd,
    psend, precv, qall, q2f,
    asend, arecv, of, orecv, xrow, xall, xf, x2,
    df, dsend, drecv, lrow, lall,
    local_sem, wq_s, wq_r, woy_s, woy_r, wor_s, wor_r, woc_s, woc_r, wf_s, wf_r, wfc_s, wfc_r,
    rs1_s, rs1_r, ag1_s, ag1_r, rs2_s, rs2_r, rs3_s, rs3_r,
    ag2_s, ag2_r, rs4_s, rs4_r, ag3_s, ag3_r,
):
    s = lax.axis_index("seq")
    r = lax.axis_index("req")
    z = s // NY
    y = s % NY
    token = y * NZ + z
    core = r % 2
    slot = core * 4 + r // 2
    sibling = (s, r + 1 - 2 * core)

    def seq_dev(zz, yy):
        return (zz * NY + yy, r)

    def req_dev(i):
        return (s, (r + i) % NR)

    rows_y = [(y + NY // 2 + k) % NY for k in range(NY)]

    def each_seq(fn):
        def line(i, carry):
            zz = (z + NZ // 2 + i) % NZ
            for yy in rows_y:
                fn(zz, yy)
            return carry

        lax.fori_loop(0, NZ // 2, line, 0)
        lax.fori_loop(NZ // 2 + 1, NZ, line, 0)
        for k, yy in enumerate(rows_y):
            if k != NY // 2:
                fn(z, yy)

    def copy(src, dst, ssem, rsem, dev):
        return pltpu.make_async_remote_copy(
            src_ref=src, dst_ref=dst, send_sem=ssem, recv_sem=rsem,
            device_id=dev, device_id_type=MESH,
        )

    def whole(ref, ssem, rsem):
        return copy(ref, ref, ssem, rsem, req_dev(1))

    pairs = [
        (hid_hbm, hid_ref),
        (again_hbm, again_ref),
        (wqkv_ref, wown),
        (wout_ref, wo.at[slot, pl.ds(y * 32, 32)]),
        (wgate_ref, wg.at[slot]),
        (wup_ref, wu.at[slot]),
        (wdown_ref, wd.at[slot]),
        (grp_hbm, grp_ref),
        (plen_hbm, plen_ref),
        (tlen_hbm, tlen_ref),
        (table_hbm, table_ref),
        (qgain_hbm, qgain_ref),
        (kgain_hbm, kgain_ref),
        (pagain_hbm, pagain_ref),
        (fgain_hbm, fgain_ref),
        (pfgain_hbm, pfgain_ref),
        (pk_ref.at[0], kbuf.at[pl.ds(0, 128)]),
        (pk_ref.at[1], kbuf.at[pl.ds(128, 128)]),
        (tk_ref.at[0], kbuf.at[pl.ds(256, 256)]),
        (pv_ref.at[0], vbuf.at[pl.ds(0, 128)]),
        (pv_ref.at[1], vbuf.at[pl.ds(128, 128)]),
        (tv_ref.at[0], vbuf.at[pl.ds(256, 256)]),
    ]
    loads = [pltpu.make_async_copy(a, b, local_sem.at[i]) for i, (a, b) in enumerate(pairs)]
    for ld in loads:
        ld.start()

    barrier = pltpu.get_barrier_semaphore()

    def greet(zz, yy):
        pl.semaphore_signal(barrier, inc=1, device_id=seq_dev(zz, yy), device_id_type=MESH)

    each_seq(greet)
    for i in range(1, NR):
        pl.semaphore_signal(barrier, inc=1, device_id=req_dev(i), device_id_type=MESH)

    def meet(dev):
        pl.semaphore_signal(barrier, inc=1, device_id=dev, device_id_type=MESH)

    for i in range(1, NR):
        meet((z * NY + r, (r + i) % NR))
        meet((z * NY + (y + i) % NY, y))
    pl.when(r != y)(lambda: meet((z * NY + r, r)))
    pl.when(r != y)(lambda: meet((s, y)))

    for ld in loads[:2]:
        ld.wait()
    for i in range(REQS):
        hf[STEPS * i : STEPS * (i + 1), :] = hid_ref[i].astype(F32)
    hidden = hf[...]
    scale = lax.rsqrt(jnp.mean(hidden * hidden, axis=1, keepdims=True) + EPSILON)
    nb[...] = (hidden * scale * again_ref[...]).astype(BF16)
    for j in range(DR):
        hid3[:, j, :] = hf[:, LANES * j : LANES * (j + 1)]

    peers = NS - 1 + NR - 1 + 2 * (NR - 1)
    pl.when(r == y)(lambda: pl.semaphore_wait(barrier, peers))
    pl.when(r != y)(lambda: pl.semaphore_wait(barrier, peers + 2))

    loads[2].wait()
    rows_here = wq.at[pl.ds(y * 32, 32)]
    for i in range(1, NR):
        copy(wown, rows_here, wq_s, wq_r, (z * NY + r, (r + i) % NR)).start()

    @pl.when(r != y)
    def _():
        copy(wown, rows_here, wq_s, wq_r, (z * NY + r, r)).start()

    @pl.when(r == y)
    def _():
        wq[pl.ds(pl.multiple_of(y * 32, 32), 32), :] = wown[...]

    x256 = nb[:, pl.ds(pl.multiple_of(z * 256, 256), 256)]

    @pl.when(r != y)
    def _():
        whole(wq, wq_s, wq_r).wait_recv()

    @pl.when(r == y)
    def _():
        whole(wq.at[pl.ds(0, 224)], wq_s, wq_r).wait_recv()

    part = jnp.dot(x256, wq[...], preferred_element_type=F32)
    for i in range(REQS):
        psend[i] = part[STEPS * i : STEPS * (i + 1), :]
    odd = y % 2
    quad = y // 2
    own_request = 2 * z + odd
    source = odd * NZ + z
    precv[source] = psend[own_request]
    for i in range(NZ):
        zz = (z + NZ // 2 + i) % NZ
        for b in range(2):
            if i == NZ // 2 and b == 0:
                continue
            other = (odd + b) % 2
            copy(
                psend.at[2 * zz + other], precv.at[source], rs1_s, rs1_r,
                seq_dev(zz, 2 * quad + other),
            ).start()

    def over_x(w, ssem, rsem):
        for i in range(1, 4):
            copy(w.at[slot], w.at[slot], ssem, rsem, (s, (r + 2 * i) % NR)).start()

    def over_core(w, ssem, rsem):
        half = w.at[pl.ds(core * 4, 4)]
        copy(half, half, ssem, rsem, sibling).start()

    for ld in loads[3:7]:
        ld.wait()
    mine = wo.at[slot, pl.ds(y * 32, 32)]
    for i in range(1, NY):
        copy(mine, mine, woy_s, woy_r, seq_dev(z, (y + i) % NY)).start()
    over_x(wg, wf_s.at[0], wf_r.at[0])

    for ld in loads[7:16]:
        ld.wait()
    req_of = iota((T, REQS), 0) // STEPS == iota((T, REQS), 1)
    group = jnp.sum(
        jnp.where(req_of, (grp_ref[...] % 2).astype(F32), 0.0), axis=1, keepdims=True
    )
    tail_len = jnp.sum(jnp.where(req_of, tlen_ref[...].astype(F32), 0.0), axis=1, keepdims=True)
    lanes = iota((T, 256), 1)
    plen = jnp.where(lanes < 128, plen_ref[:, 0:1], plen_ref[:, 1:2])
    prompt_live = (s * 128 + lanes % 128 < plen) & (group == (lanes // 128).astype(F32))
    match = (table_ref[...] == s * 16 + iota((256, 1024), 0) // PAGE).astype(F32).astype(BF16)
    entry = iota((8, 1024), 1)
    digits = jnp.where(iota((8, 1024), 0) == 0, entry // 64, entry % 64)
    found = lax.dot_general(
        digits.astype(F32).astype(BF16), match, NT, preferred_element_type=F32
    )
    owner = found[0:1, :]
    position = found[1:2, :] * PAGE + (iota((1, 256), 1) % PAGE).astype(F32)
    own_req = (iota((T, 256), 0) // STEPS).astype(F32)
    tail_live = (owner == own_req) & (position < tail_len)
    maskf[:, 0:256] = jnp.where(prompt_live, 1.0, 0.0)
    maskf[:, 256:512] = jnp.where(tail_live, 1.0, 0.0)

    whole(precv.at[pl.ds(0, REQS - 1)], rs1_s, rs1_r).wait_recv()
    low = jnp.sum(precv[0:NZ], axis=0)
    high = jnp.sum(precv[NZ : 2 * NZ], axis=0)
    chunks = [low[:, LANES * u : LANES * (u + 1)] for u in range(3)]
    chunks += [high[:, LANES * u : LANES * (u + 1)] for u in range(3)]
    pieces = []
    for i in range(3):
        pair = chunks[2 * i : 2 * i + 2]
        mean = sum(jnp.sum(c * c, axis=1, keepdims=True) for c in pair) / HD
        inverse = lax.rsqrt(mean + EPSILON)
        head = 3 * quad + i
        for u in range(2):
            gain = jnp.where(
                head < H,
                qgain_ref[u : u + 1, :],
                jnp.where(head < H + KV, kgain_ref[u : u + 1, :], 1.0),
            )
            pieces.append(pair[u] * inverse * gain)
    place = own_request * 4 + quad
    qall[place] = jnp.concatenate(pieces, axis=1).astype(BF16)

    def send_ag1(zz, yy):
        copy(qall.at[place], qall.at[place], ag1_s, ag1_r, seq_dev(zz, yy)).start()

    each_seq(send_ag1)
    whole(wo.at[0, pl.ds(0, 224)], woy_s, woy_r).wait_recv()
    over_x(wo, wor_s, wor_r)
    over_x(wu, wf_s.at[1], wf_r.at[1])
    over_x(wd, wf_s.at[2], wf_r.at[2])
    for ld in loads[16:]:
        ld.wait()
    whole(qall.at[pl.ds(0, NS - 1)], ag1_s, ag1_r).wait_recv()
    for i in range(REQS):
        for k in range(4):
            block = qall[4 * i + k].astype(F32)
            for u in range(3):
                top = T * (3 * k + u) + STEPS * i
                q2f[top : top + STEPS, :] = block[:, HD * u : HD * (u + 1)]

    mask = maskf[...]
    mask4 = jnp.concatenate([mask, mask, mask, mask], axis=0) > 0.5
    rows = H // KV * T
    for c in range(KV):
        heads = q2f[rows * c : rows * (c + 1), :].astype(BF16)
        scores = lax.dot_general(
            heads, kbuf[:, HD * c : HD * (c + 1)], NT, preferred_element_type=F32
        )
        scores = jnp.where(mask4, scores, NEGATIVE)
        top = jnp.max(scores, axis=1, keepdims=True)
        probs = jnp.where(mask4, jnp.exp(scores - top), 0.0)
        total = jnp.sum(probs, axis=1, keepdims=True)
        accum = jnp.dot(
            probs.astype(BF16), vbuf[:, HD * c : HD * (c + 1)], preferred_element_type=F32
        )
        lane = iota((rows, LANES), 1)
        stats = jnp.zeros((rows, LANES), F32)
        for base, rest in ((0, top), (3, total)):
            for k in range(3):
                high = rest.astype(BF16).astype(F32)
                stats = jnp.where(lane == base + k, high, stats)
                rest = rest - high
        eight = rows // 8
        asend[eight * c : eight * (c + 1), :, 0:HD] = accum.reshape(eight, 8, HD).astype(BF16)
        asend[eight * c : eight * (c + 1), :, HD : HD + LANES] = stats.reshape(
            eight, 8, LANES
        ).astype(BF16)

    arecv[s] = asend[s]

    def send_rs2(zz, yy):
        copy(asend.at[zz * NY + yy], arecv.at[s], rs2_s, rs2_r, seq_dev(zz, yy)).start()

    each_seq(send_rs2)
    whole(wo.at[pl.ds(0, 3)], wor_s, wor_r).wait_recv()
    over_core(wo, woc_s, woc_r)
    for k, w in enumerate((wg, wu, wd)):
        whole(w.at[pl.ds(0, 3)], wf_s.at[k], wf_r.at[k]).wait_recv()
        over_core(w, wfc_s.at[k], wfc_r.at[k])

    def eight_of(head):
        return q2f[pl.ds(pl.multiple_of(head * T + y * 8, 8), 8), :]

    q8 = eight_of(z).astype(BF16)
    k8 = eight_of(H + z // 4).astype(BF16)
    v8 = eight_of(H + KV + z // 4)
    new_scores = lax.dot_general(q8, k8, NT, preferred_element_type=F32)
    qi = iota((8, 8), 0)
    ki = iota((8, 8), 1)
    causal = (qi // STEPS == ki // STEPS) & (ki <= qi)
    new_scores = jnp.where(causal, new_scores, NEGATIVE)
    new_top = jnp.max(new_scores, axis=1, keepdims=True)

    whole(arecv.at[pl.ds(0, NS - 1)], rs2_s, rs2_r).wait_recv()
    stats = arecv[:, :, HD : HD + LANES].astype(F32)
    tops = stats[:, :, 0:1] + stats[:, :, 1:2] + stats[:, :, 2:3]
    totals = stats[:, :, 3:4] + stats[:, :, 4:5] + stats[:, :, 5:6]
    highest = jnp.maximum(jnp.max(tops, axis=0), new_top)
    weight = jnp.exp(tops - highest[None])
    new_probs = jnp.where(causal, jnp.exp(new_scores - highest), 0.0)
    denominator = jnp.sum(totals * weight, axis=0) + jnp.sum(new_probs, axis=1, keepdims=True)
    numerator = jnp.sum(arecv[:, :, 0:HD].astype(F32) * weight, axis=0) + jnp.dot(
        new_probs, v8, preferred_element_type=F32, precision=lax.Precision.HIGHEST
    )
    attention = (numerator / denominator).astype(BF16)

    whole(wo.at[pl.ds(0, 4)], woc_s, woc_r).wait_recv()
    for k in range(NR):
        part = jnp.dot(attention, wo[k % 2 * 4 + k // 2], preferred_element_type=F32)
        for u in range(2):
            of[:, 2 * k + u, :] = part[:, LANES * u : LANES * (u + 1)]
    orecv[z] = of[z]
    for i in range(1, NZ):
        zz = (z + i) % NZ
        copy(of.at[zz], orecv.at[z], rs3_s, rs3_r, seq_dev(zz, y)).start()
    whole(orecv.at[pl.ds(0, NZ - 1)], rs3_s, rs3_r).wait_recv()
    out_row = jnp.sum(orecv[...], axis=0)
    residual = hid3[token] + row_norm(out_row) * pagain_ref[...]
    xrow[...] = (row_norm(residual) * fgain_ref[...]).astype(BF16)
    xall[token] = xrow[...]

    def send_ag2(zz, yy):
        copy(xrow, xall.at[token], ag2_s, ag2_r, seq_dev(zz, yy)).start()

    each_seq(send_ag2)
    for k, w in enumerate((wg, wu, wd)):
        whole(w.at[pl.ds(0, 4)], wfc_s.at[k], wfc_r.at[k]).wait_recv()
    whole(xall.at[pl.ds(0, NS - 1)], ag2_s, ag2_r).wait_recv()

    xf[...] = xall[...].astype(F32)
    for j in range(DR):
        x2[:, LANES * j : LANES * (j + 1)] = xf[:, j, :].astype(BF16)
    gate = jnp.zeros((T, LANES), F32)
    up = jnp.zeros((T, LANES), F32)
    for k in range(NR):
        xk = x2[:, 256 * k : 256 * (k + 1)]
        gate = gate + jnp.dot(xk, wg[k % 2 * 4 + k // 2], preferred_element_type=F32)
        up = up + jnp.dot(xk, wu[k % 2 * 4 + k // 2], preferred_element_type=F32)
    activated = (jax.nn.gelu(gate, approximate=True) * up).astype(BF16)
    for k in range(NR):
        part = jnp.dot(activated, wd[k % 2 * 4 + k // 2], preferred_element_type=F32)
        for u in range(2):
            df[:, 2 * k + u, :] = part[:, LANES * u : LANES * (u + 1)]
    dsend[...] = df[...].astype(BF16)
    drecv[s] = dsend[token]

    def send_rs4(zz, yy):
        copy(dsend.at[yy * NZ + zz], drecv.at[s], rs4_s, rs4_r, seq_dev(zz, yy)).start()

    each_seq(send_rs4)
    whole(drecv.at[pl.ds(0, NS - 1)], rs4_s, rs4_r).wait_recv()
    down = jnp.sum(drecv[...].astype(F32), axis=0)
    lrow[...] = (residual + row_norm(down) * pfgain_ref[...]).astype(BF16)
    lall[token] = lrow[...]

    def send_ag3(zz, yy):
        copy(lrow, lall.at[token], ag3_s, ag3_r, seq_dev(zz, yy)).start()

    each_seq(send_ag3)

    whole(wq.at[pl.ds(0, 224)], wq_s, wq_r).wait_send()
    pl.when(r != y)(lambda: whole(wq.at[pl.ds(0, 32)], wq_s, wq_r).wait_send())
    whole(wo.at[0, pl.ds(0, 224)], woy_s, woy_r).wait_send()
    whole(wo.at[pl.ds(0, 3)], wor_s, wor_r).wait_send()
    whole(wo.at[pl.ds(0, 4)], woc_s, woc_r).wait_send()
    for k, w in enumerate((wg, wu, wd)):
        whole(w.at[pl.ds(0, 3)], wf_s.at[k], wf_r.at[k]).wait_send()
        whole(w.at[pl.ds(0, 4)], wfc_s.at[k], wfc_r.at[k]).wait_send()
    whole(precv.at[pl.ds(0, REQS - 1)], rs1_s, rs1_r).wait_send()
    whole(qall.at[pl.ds(0, NS - 1)], ag1_s, ag1_r).wait_send()
    whole(arecv.at[pl.ds(0, NS - 1)], rs2_s, rs2_r).wait_send()
    whole(orecv.at[pl.ds(0, NZ - 1)], rs3_s, rs3_r).wait_send()
    whole(xall.at[pl.ds(0, NS - 1)], ag2_s, ag2_r).wait_send()
    whole(drecv.at[pl.ds(0, NS - 1)], rs4_s, rs4_r).wait_send()

    whole(lall.at[pl.ds(0, NS - 1)], ag3_s, ag3_r).wait_recv()
    xf[...] = lall[...].astype(F32)
    for j in range(DR):
        out_ref[:, LANES * j : LANES * (j + 1)] = xf[:, j, :].astype(BF16)
    whole(lall.at[pl.ds(0, NS - 1)], ag3_s, ag3_r).wait_send()


def on_device(
    hidden_in, attn_gain, q_gain, k_gain, post_attn_gain, ffn_gain, post_ffn_gain,
    w_qkv, w_out, w_gate, w_up, w_down,
    prompt_keys, prompt_values, tail_keys, tail_values,
    group_of, prompt_lengths, tail_lengths, page_table,
):
    vmem = pl.BlockSpec(memory_space=pltpu.VMEM)
    hbm = pl.BlockSpec(memory_space=pltpu.HBM)
    dma = pltpu.SemaphoreType.DMA
    scratch = [
        pltpu.VMEM((REQS, STEPS, D), BF16),
        pltpu.VMEM((1, D), F32),
        pltpu.VMEM((2, LANES), F32),
        pltpu.VMEM((2, LANES), F32),
        pltpu.VMEM((DR, LANES), F32),
        pltpu.VMEM((DR, LANES), F32),
        pltpu.VMEM((DR, LANES), F32),
        pltpu.VMEM((1, REQS), jnp.int32),
        pltpu.VMEM((1, 2), jnp.int32),
        pltpu.VMEM((1, REQS), jnp.int32),
        pltpu.VMEM((1, 1024), jnp.int32),
        pltpu.VMEM((T, D), F32),
        pltpu.VMEM((T, DR, LANES), F32),
        pltpu.VMEM((T, D), BF16),
        pltpu.VMEM((512, 512), BF16),
        pltpu.VMEM((512, 512), BF16),
        pltpu.VMEM((T, 512), F32),
        pltpu.VMEM((32, 384), BF16),
        pltpu.VMEM((256, 384), BF16),
        pltpu.VMEM((NR, 256, 256), BF16),
        pltpu.VMEM((NR, 256, LANES), BF16),
        pltpu.VMEM((NR, 256, LANES), BF16),
        pltpu.VMEM((NR, LANES, 256), BF16),
        pltpu.VMEM((REQS, STEPS, 384), F32),
        pltpu.VMEM((REQS, STEPS, 384), F32),
        pltpu.VMEM((NS, STEPS, 768), BF16),
        pltpu.VMEM((12 * T, HD), F32),
        pltpu.VMEM((NS, 8, HD + LANES), BF16),
        pltpu.VMEM((NS, 8, HD + LANES), BF16),
        pltpu.VMEM((NZ, DR, LANES), F32),
        pltpu.VMEM((NZ, DR, LANES), F32),
        pltpu.VMEM((DR, LANES), BF16),
        pltpu.VMEM((T, DR, LANES), BF16),
        pltpu.VMEM((T, DR, LANES), F32),
        pltpu.VMEM((T, D), BF16),
        pltpu.VMEM((T, DR, LANES), F32),
        pltpu.VMEM((T, DR, LANES), BF16),
        pltpu.VMEM((NS, DR, LANES), BF16),
        pltpu.VMEM((DR, LANES), BF16),
        pltpu.VMEM((T, DR, LANES), BF16),
        dma((22,)),
        dma, dma, dma, dma, dma, dma, dma, dma, dma((3,)), dma((3,)), dma((3,)), dma((3,)),
        dma, dma, dma, dma, dma, dma, dma, dma,
        dma, dma, dma, dma, dma, dma,
    ]
    out = pl.pallas_call(
        kernel,
        name="decode_layer",
        out_shape=jax.ShapeDtypeStruct((T, D), BF16),
        in_specs=[hbm] * 20,
        out_specs=vmem,
        scratch_shapes=scratch,
        compiler_params=pltpu.CompilerParams(
            collective_id=0, has_side_effects=True, vmem_limit_bytes=40 << 20
        ),
    )(*[pltpu.with_memory_space_constraint(a, pltpu.HBM) for a in (
        hidden_in,
        attn_gain.reshape(1, D),
        q_gain.reshape(2, LANES),
        k_gain.reshape(2, LANES),
        post_attn_gain.reshape(DR, LANES),
        ffn_gain.reshape(DR, LANES),
        post_ffn_gain.reshape(DR, LANES),
        w_qkv, w_out, w_gate, w_up, w_down,
        prompt_keys, prompt_values, tail_keys, tail_values,
        group_of.reshape(1, REQS),
        prompt_lengths.reshape(1, 2),
        tail_lengths.reshape(1, REQS),
        page_table,
    )])
    return out.reshape(REQS, STEPS, D)


def solution(mesh):
    return jax.shard_map(
        on_device,
        mesh=mesh,
        in_specs=(
            P("req", None, None),
            P(), P(), P(), P(), P(), P(),
            P("seq", "req"),
            P("seq", "req"),
            P("req", "seq"),
            P("req", "seq"),
            P("seq", "req"),
            P("req", "seq", None),
            P("req", "seq", None),
            P("req", "seq", None),
            P("req", "seq", None),
            P("req"), P("req"), P("req"),
            P("req", None),
        ),
        out_specs=P("req", None, None),
        check_vma=False,
    )
```

time: 1220 us -> 99.3 us (0.08)
  the two profiles are of different devices: /device:TPU:6 before, /device:TPU:4 now
where the time goes in v1:
time: 99.3 us; the launch traced here: 99.2 us
  Pallas kernels  98.4 us (99%)
    pallas_call x1, Pallas kernels, on_device(): pl.pallas_call(kernel, name='decode_layer', out_shape=jax.ShapeDtypeStruc...  98.4 us

profile of v1, /device:TPU:4, one launch (start us, length us, event | category | flops | bytes accessed | tf_op | source)
XLA Modules:
  0.0 99.2 jit_solution(6713352755552539644)
XLA Ops:
  0.0 98.4 %decode_layer.1 = bf16[64,2048]{1,0:T(8,128)(2,1)S(1)} custom-call(bf16[16,4,2048]{2,1,0:T(4,128)(2,1)} %hid_hbm.1, f32[1,2048]{1,0:T(1,128)} %bitcast.9, f32[2,128]{1,0:T(2,128)} %bitcast.13, f32[2,128]{1,0:T(2,128)} %bitcast.14, f32[16,128]{1,0:T(8,128)} %bitcast.10, f32[16,128]{1,0:T(8,128)} %bitcast.11, f32[16,128]{1,0:T(8,128)} %bitcast.12, ...), custom_call_target="tpu_custom_call" | custom-call | tf_op jit(solution)/shard_map/decode_layer/pallas_call | solution.py:473
  98.4 0.8 reshape.39

commit v2 on v1

--- a/solution.py
+++ b/solution.py
@@ -60,6 +60,7 @@
     z = s // NY
     y = s % NY
     token = y * NZ + z
+    chunk = (y + r) % NY
     core = r % 2
     slot = core * 4 + r // 2
     sibling = (s, r + 1 - 2 * core)
@@ -124,21 +125,24 @@
 
     barrier = pltpu.get_barrier_semaphore()
 
-    def greet(zz, yy):
-        pl.semaphore_signal(barrier, inc=1, device_id=seq_dev(zz, yy), device_id_type=MESH)
-
-    each_seq(greet)
-    for i in range(1, NR):
-        pl.semaphore_signal(barrier, inc=1, device_id=req_dev(i), device_id_type=MESH)
-
     def meet(dev):
         pl.semaphore_signal(barrier, inc=1, device_id=dev, device_id_type=MESH)
 
+    partner = (chunk + 1 - 2 * (chunk % 2) + NR - r) % NY
+    for i in range(1, NY):
+        meet(seq_dev(z, (y + i) % NY))
+        meet(seq_dev((z + i) % NZ, y))
+    for i in range(NZ):
+        meet(seq_dev((z + i) % NZ, partner))
+    for i in range(1, 4):
+        meet((s, (r + 2 * i) % NR))
+    meet(sibling)
+
     for i in range(1, NR):
-        meet((z * NY + r, (r + i) % NR))
-        meet((z * NY + (y + i) % NY, y))
-    pl.when(r != y)(lambda: meet((z * NY + r, r)))
-    pl.when(r != y)(lambda: meet((s, y)))
+        meet((z * NY + NY - i, (r + i) % NR))
+        meet((z * NY + (y + i) % NY, chunk))
+    pl.when(y != 0)(lambda: meet((z * NY, r)))
+    pl.when(y != 0)(lambda: meet((s, chunk)))
 
     for ld in loads[:2]:
         ld.wait()
@@ -150,38 +154,38 @@
     for j in range(DR):
         hid3[:, j, :] = hf[:, LANES * j : LANES * (j + 1)]
 
-    peers = NS - 1 + NR - 1 + 2 * (NR - 1)
-    pl.when(r == y)(lambda: pl.semaphore_wait(barrier, peers))
-    pl.when(r != y)(lambda: pl.semaphore_wait(barrier, peers + 2))
+    peers = 2 * (NY - 1) + NZ + 4 + 2 * (NR - 1)
+    pl.when(y == 0)(lambda: pl.semaphore_wait(barrier, peers))
+    pl.when(y != 0)(lambda: pl.semaphore_wait(barrier, peers + 2))
 
     loads[2].wait()
     rows_here = wq.at[pl.ds(y * 32, 32)]
     for i in range(1, NR):
-        copy(wown, rows_here, wq_s, wq_r, (z * NY + r, (r + i) % NR)).start()
-
-    @pl.when(r != y)
+        copy(wown, rows_here, wq_s, wq_r, (z * NY + NY - i, (r + i) % NR)).start()
+
+    @pl.when(y != 0)
     def _():
-        copy(wown, rows_here, wq_s, wq_r, (z * NY + r, r)).start()
-
-    @pl.when(r == y)
+        copy(wown, rows_here, wq_s, wq_r, (z * NY, r)).start()
+
+    @pl.when(y == 0)
     def _():
         wq[pl.ds(pl.multiple_of(y * 32, 32), 32), :] = wown[...]
 
     x256 = nb[:, pl.ds(pl.multiple_of(z * 256, 256), 256)]
 
-    @pl.when(r != y)
+    @pl.when(y != 0)
     def _():
         whole(wq, wq_s, wq_r).wait_recv()
 
-    @pl.when(r == y)
+    @pl.when(y == 0)
     def _():
         whole(wq.at[pl.ds(0, 224)], wq_s, wq_r).wait_recv()
 
     part = jnp.dot(x256, wq[...], preferred_element_type=F32)
     for i in range(REQS):
         psend[i] = part[STEPS * i : STEPS * (i + 1), :]
-    odd = y % 2
-    quad = y // 2
+    odd = chunk % 2
+    quad = chunk // 2
     own_request = 2 * z + odd
     source = odd * NZ + z
     precv[source] = psend[own_request]
@@ -193,7 +197,7 @@
             other = (odd + b) % 2
             copy(
                 psend.at[2 * zz + other], precv.at[source], rs1_s, rs1_r,
-                seq_dev(zz, 2 * quad + other),
+                seq_dev(zz, (2 * quad + other + NR - r) % NY),
             ).start()
 
     def over_x(w, ssem, rsem):
@@ -394,7 +398,7 @@
     each_seq(send_ag3)
 
     whole(wq.at[pl.ds(0, 224)], wq_s, wq_r).wait_send()
-    pl.when(r != y)(lambda: whole(wq.at[pl.ds(0, 32)], wq_s, wq_r).wait_send())
+    pl.when(y != 0)(lambda: whole(wq.at[pl.ds(0, 32)], wq_s, wq_r).wait_send())
     whole(wo.at[0, pl.ds(0, 224)], woy_s, woy_r).wait_send()
     whole(wo.at[pl.ds(0, 3)], wor_s, wor_r).wait_send()
     whole(wo.at[pl.ds(0, 4)], woc_s, woc_r).wait_send()

time: 99.3 us -> 90 us (0.906)
  the two profiles are of different devices: /device:TPU:4 before, /device:TPU:8 now
where the time goes in v2:
time: 90 us; the launch traced here: 89.8 us
  Pallas kernels  89 us (99%)
    pallas_call x1, Pallas kernels, on_device(): pl.pallas_call(kernel, name='decode_layer', out_shape=jax.ShapeDtypeStruc...  89 us

profile of v2, /device:TPU:8, one launch (start us, length us, event | category | flops | bytes accessed | tf_op | source)
XLA Modules:
  0.0 89.8 jit_solution(5926852371076479383)
XLA Ops:
  0.0 89.0 %decode_layer.1 = bf16[64,2048]{1,0:T(8,128)(2,1)S(1)} custom-call(bf16[16,4,2048]{2,1,0:T(4,128)(2,1)} %hid_hbm.1, f32[1,2048]{1,0:T(1,128)} %bitcast.9, f32[2,128]{1,0:T(2,128)} %bitcast.13, f32[2,128]{1,0:T(2,128)} %bitcast.14, f32[16,128]{1,0:T(8,128)} %bitcast.10, f32[16,128]{1,0:T(8,128)} %bitcast.11, f32[16,128]{1,0:T(8,128)} %bitcast.12, ...), custom_call_target="tpu_custom_call" | custom-call | tf_op jit(solution)/shard_map/decode_layer/pallas_call | solution.py:477
  89.0 0.8 reshape.39

commit v3 on v2

--- a/solution.py
+++ b/solution.py
@@ -71,7 +71,7 @@
     def req_dev(i):
         return (s, (r + i) % NR)
 
-    rows_y = [(y + NY // 2 + k) % NY for k in range(NY)]
+    rows_y = [(y + k) % NY for k in (4, 3, 5, 2, 0, 6, 1, 7)]
 
     def each_seq(fn):
         def line(i, carry):
@@ -80,8 +80,9 @@
                 fn(zz, yy)
             return carry
 
-        lax.fori_loop(0, NZ // 2, line, 0)
+        lax.fori_loop(0, NZ // 2 - 1, line, 0)
         lax.fori_loop(NZ // 2 + 1, NZ, line, 0)
+        line(NZ // 2 - 1, 0)
         for k, yy in enumerate(rows_y):
             if k != NY // 2:
                 fn(z, yy)

time: 90 us -> 87.5 us (0.972)
  Pallas kernels: 89 us -> 86.5 us
    pallas_call x1, Pallas kernels: 89 us -> 86.5 us  [on_device(): pl.pallas_call(kernel, name='decode_layer', out_shape=jax.ShapeDtypeStruc...]
where the time goes in v3:
time: 87.5 us; the launch traced here: 87.3 us
  Pallas kernels  86.5 us (99%)
    pallas_call x1, Pallas kernels, on_device(): pl.pallas_call(kernel, name='decode_layer', out_shape=jax.ShapeDtypeStruc...  86.5 us

profile of v3, /device:TPU:8, one launch (start us, length us, event | category | flops | bytes accessed | tf_op | source)
XLA Modules:
  0.0 87.3 jit_solution(13737864763991905112)
XLA Ops:
  0.0 86.5 %decode_layer.1 = bf16[64,2048]{1,0:T(8,128)(2,1)S(1)} custom-call(bf16[16,4,2048]{2,1,0:T(4,128)(2,1)} %hid_hbm.1, f32[1,2048]{1,0:T(1,128)} %bitcast.9, f32[2,128]{1,0:T(2,128)} %bitcast.13, f32[2,128]{1,0:T(2,128)} %bitcast.14, f32[16,128]{1,0:T(8,128)} %bitcast.10, f32[16,128]{1,0:T(8,128)} %bitcast.11, f32[16,128]{1,0:T(8,128)} %bitcast.12, ...), custom_call_target="tpu_custom_call" | custom-call | tf_op jit(solution)/shard_map/decode_layer/pallas_call | solution.py:478
  86.5 0.8 reshape.39
